TPU v7x, 128 devices: a whole 4x4x4 slice. The times are simulated.
128 devices in a mesh: frame: 16 (over y, x), tensor: 8 (over z, core).
Axes of the slice: x: 4, y: 4, z: 4, core: 2. Of those that a mesh axis runs over, the one named last changes fastest.
Arguments:
- latents: bfloat16 [8192, 5120], P('frame', 'tensor'), may hold values from -6 to 6
- w_query: bfloat16 [5120, 3072], P(None, 'tensor'), may hold values from -0.078125 to 0.078125
- w_key: bfloat16 [5120, 3072], P(None, 'tensor'), may hold values from -0.078125 to 0.078125
- w_value: bfloat16 [5120, 3072], P(None, 'tensor'), may hold values from -0.078125 to 0.078125
- w_out: bfloat16 [3072, 5120], P('tensor'), may hold values from -0.109375 to 0.109375
- query_gain: float32 [24, 128], P('tensor'), may hold values from 0.5 to 14, as said below
- key_gain: float32 [24, 128], P('tensor'), may hold values from 0.5 to 14, as said below
- mod_table: float32 [16, 3, 5120], replicated, may hold values from -3 to 3
- levels: int32 [16], P('frame'), may hold values from 0 to 15
- span_counts: int32 [16], replicated, may hold values from 1 to 512, 6144 in all
- block_mask: int32 [16, 16], P('frame'), may hold values 0 or 1
- span_order: int32 [16], replicated, may hold values from 0 to 15, each once
Outputs:
- updated: bfloat16 [8192, 5120], P('frame', 'tensor')
Inputs may be any that keep to these rules, and one draw needn't show every extreme that they name: `query_gain`: gains are positive. `key_gain`: gains are positive. `span_order`: each rank appears once.
All inputs are finite; a program needn't handle non-finite values. No bound on the sum of `block_mask` on one device may be relied on, other than what follows from the above.
Results may differ from a plain program's by a relative error of at most 0.012.
The roundings to bfloat16 on the way count: a program that leaves them out, or rounds other values in their place, can miss the bound.
Values may be sent and summed in bfloat16 or wider, within the bound.
No kernel may reach another device: no remote copies, remote signals or barrier semaphores. Data moves between devices by JAX's collectives and lax.ppermute only.
A program may use at most 128 MiB of HBM per device.

v0:
```python
import math
import jax
import jax.numpy as jnp
from jax import lax
from jax.sharding import PartitionSpec as P

HEAD_DIM = 128
EPSILON = 1e-06
NEG_FILL = -1e30


def on_device(
    latents,
    w_query,
    w_key,
    w_value,
    w_out,
    query_gain,
    key_gain,
    mod_table,
    levels,
    span_counts,
    block_mask,
    span_order,
):
    row_count = latents.shape[0]
    shard_width = latents.shape[1]
    span_total = lax.axis_size("frame")
    my_span = lax.axis_index("frame")
    column_start = lax.axis_index("tensor") * shard_width
    selector = jnp.arange(mod_table.shape[0], dtype=jnp.int32) == levels[0]
    modulation = jnp.sum(jnp.where(selector[:, None, None], mod_table, 0.0), axis=0)
    shift_row = modulation[0]
    scale_row = modulation[1]
    gate_row = modulation[2]
    whole = lax.all_gather(latents, "tensor", axis=1, tiled=True).astype(jnp.float32)
    row_mean = jnp.mean(whole, axis=1, keepdims=True)
    row_square = jnp.mean(whole * whole, axis=1, keepdims=True)
    normed = (
        (whole - row_mean)
        * lax.rsqrt(row_square - row_mean * row_mean + EPSILON)
        * (1.0 + scale_row)
        + shift_row
    ).astype(jnp.bfloat16)
    head_local = w_query.shape[1] // HEAD_DIM

    def project(weight, gain_table):
        shaped = jnp.dot(normed, weight, preferred_element_type=jnp.float32).reshape(
            row_count, head_local, HEAD_DIM
        )
        scaled = (
            shaped
            * lax.rsqrt(jnp.mean(shaped * shaped, axis=-1, keepdims=True) + EPSILON)
            * gain_table
        )
        return scaled.astype(jnp.bfloat16)

    queries = project(w_query, query_gain)
    keys_local = project(w_key, key_gain).reshape(row_count, head_local * HEAD_DIM)
    values_local = jnp.dot(normed, w_value, preferred_element_type=jnp.float32).astype(jnp.bfloat16)
    kv_pair = jnp.stack((keys_local, values_local))
    span_ids = jnp.arange(span_total, dtype=jnp.int32)
    my_rank = jnp.sum(jnp.where(span_ids == my_span, span_order, 0))
    mask_row = block_mask[0]
    slot_index = jnp.arange(row_count, dtype=jnp.int32)
    score_factor = 1.0 / math.sqrt(HEAD_DIM)
    initial = (
        jnp.full((head_local, row_count), NEG_FILL, jnp.float32),
        jnp.zeros((head_local, row_count), jnp.float32),
        jnp.zeros((head_local, row_count, HEAD_DIM), jnp.float32),
    )
    piece = lax.all_gather(kv_pair, "frame", axis=1, tiled=True)
    block_count = piece.shape[1] // row_count
    key_blocks = piece[0].reshape(block_count, row_count, head_local, HEAD_DIM)
    value_blocks = piece[1].reshape(block_count, row_count, head_local, HEAD_DIM)

    def fold_block(running, block):
        key_block, value_block, block_index = block
        source_count = jnp.sum(jnp.where(span_ids == block_index, span_counts, 0))
        linked = jnp.sum(jnp.where(span_ids == block_index, mask_row, 0)) == 1
        source_rank = jnp.sum(jnp.where(span_ids == block_index, span_order, 0))
        allowed = (source_rank <= my_rank) & (linked | (block_index == my_span))
        valid = allowed & (slot_index < source_count)
        running_max, running_sum, accum = running
        scores = (
            jnp.einsum("qhd,khd->hqk", queries, key_block, preferred_element_type=jnp.float32)
            * score_factor
        )
        scores = jnp.where(valid[None, None, :], scores, NEG_FILL)
        new_max = jnp.maximum(running_max, jnp.max(scores, axis=-1))
        weights = jnp.where(valid[None, None, :], jnp.exp(scores - new_max[:, :, None]), 0.0)
        factor = jnp.exp(running_max - new_max)
        new_sum = running_sum * factor + jnp.sum(weights, axis=-1)
        new_accum = accum * factor[:, :, None] + jnp.einsum(
            "hqk,khd->hqd",
            weights.astype(jnp.bfloat16),
            value_block,
            preferred_element_type=jnp.float32,
        )
        return ((new_max, new_sum, new_accum), None)

    blocks = (key_blocks, value_blocks, jnp.arange(block_count, dtype=jnp.int32))
    result, unused = lax.scan(fold_block, initial, blocks)
    running_max, running_sum, accum = result
    attended = (accum / running_sum[:, :, None]).astype(jnp.bfloat16)
    attended = jnp.transpose(attended, (1, 0, 2)).reshape(row_count, head_local * HEAD_DIM)
    partial_out = jnp.dot(attended, w_out, preferred_element_type=jnp.float32)
    projected = lax.psum_scatter(
        partial_out.astype(jnp.bfloat16), "tensor", scatter_dimension=1, tiled=True
    ).astype(jnp.float32)
    gate_part = lax.dynamic_slice_in_dim(gate_row, column_start, shard_width)
    return (latents.astype(jnp.float32) + gate_part * projected).astype(jnp.bfloat16)


def solution(mesh):
    return jax.shard_map(
        on_device,
        mesh=mesh,
        in_specs=(
            P("frame", "tensor"),
            P(None, "tensor"),
            P(None, "tensor"),
            P(None, "tensor"),
            P("tensor", None),
            P("tensor", None),
            P("tensor", None),
            P(),
            P("frame"),
            P(),
            P("frame", None),
            P(),
        ),
        out_specs=P("frame", "tensor"),
        check_vma=False,
    )
```

profile of v0, /device:TPU:0, one launch (start us, length us, event | category | flops | bytes accessed | tf_op | source)
XLA Modules:
  0.0 428.1 jit_solution(2990120822217263245)
XLA Ops:
  9.5 38.7 %all-gather.3.cloned.1.call-done = bf16[512,5120]{1,0:T(8,128)(2,1)} async-done(((bf16[512,640]{1,0:T(8,128)(2,1)}), bf16[512,5120]{1,0:T(8,128)(2,1)}) %all-gather.3.cloned.1.call-update) | async-done | bytes 5242896 | tf_op jit(solution)/shard_map/all_gather | solution.py:36
  48.2 4.2 convert_reduce_fusion
  52.4 3.0 fusion.28
  55.5 2.2 fusion.30
  59.5 2.2 fusion.36
  63.9 5.9 %fusion.37 = f32[512,384]{0,1:T(8,128)S(1)} fusion(bf16[512,5120]{1,0:T(8,128)(2,1)} %copy-done.1, bf16[5120,384]{1,0:T(8,128)(2,1)} %param.15), kind=kOutput, calls=%fused_computation.65 | convolution fusion | flops 2013265920 | bytes 9961472 | tf_op jit(solution)/shard_map/dot_general | solution.py:48
  70.5 90.9 %all-gather.5.cloned.1.call-done = bf16[2,8192,384]{1,2,0:T(8,128)(2,1)} async-done(((bf16[2,512,384]{1,2,0:T(8,128)(2,1)}), bf16[2,8192,384]{1,2,0:T(8,128)(2,1)}) %all-gather.5.cloned.1.call-update) | async-done | bytes 12582928 | tf_op jit(solution)/shard_map/all_gather | solution.py:72
  161.4 8.2 %fusion.34 = (bf16[1,8192,384]{1,2,0:T(8,128)(2,1)S(1)}, bf16[1,8192,384]{1,2,0:T(8,128)(2,1)}) fusion(bf16[2,8192,384]{1,2,0:T(8,128)(2,1)} %all-gather.5.cloned.1.call-done), kind=kLoop, calls=%fused_computation.62 | loop fusion | bytes 25165824 | tf_op jit(solution)/shard_map/slice | solution.py:75
  169.6 5.6 %copy.35 = bf16[48,8,16,512]{3,2,1,0:T(8,128)(2,1)} copy(bf16[48,8,16,512]{3,1,2,0:T(8,128)(2,1)S(1)} %bitcast.83) | data formatting | bytes 12582912
  175.1 9.1 %copy.28 = bf16[16,512,3,128]{3,1,2,0:T(8,128)(2,1)} copy(bf16[16,512,3,128]{1,0,3,2:T(8,128)(2,1)} %bitcast.80) | data formatting | bytes 12582912
  184.3 8.3 %copy.34 = bf16[48,8,16,512]{3,2,1,0:T(8,128)(2,1)} copy(bf16[48,8,16,512]{3,1,2,0:T(8,128)(2,1)} %bitcast.82) | data formatting | bytes 12582912
  192.6 9.2 %copy.27 = bf16[16,512,3,128]{3,1,2,0:T(8,128)(2,1)} copy(bf16[16,512,3,128]{1,0,3,2:T(8,128)(2,1)} %bitcast.81) | data formatting | bytes 12582912
  201.8 162.4 %while.17 = (s32[]{:T(128)}, f32[3,512]{1,0:T(4,128)S(1)}, f32[3,512]{1,0:T(4,128)S(1)}, f32[3,512,128]{2,1,0:T(8,128)S(1)}, s32[16]{0:T(128)S(1)}, /*index=5*/s...) while((s32[]{:T(128)}, f32[3,512]{1,0:T(4,128)S(1)}, ...), condition=%wide.region_12.13_spmd.clone.clone, body=%wide.region_6.12_spmd.clone.clone.sunk | while | flops 413475456 | bytes 12295147 | solution.py:103
  206.9 1.6 bitcast_reduce_fusion.2
  209.4 2.4 fusion.60
  217.1 1.6 bitcast_reduce_fusion.2
  219.6 2.4 fusion.60
  227.2 1.6 bitcast_reduce_fusion.2
  229.7 2.4 fusion.60
  237.4 1.6 bitcast_reduce_fusion.2
  239.9 2.4 fusion.60
  247.5 1.6 bitcast_reduce_fusion.2
  250.0 2.4 fusion.60
  257.7 1.6 bitcast_reduce_fusion.2
  260.2 2.4 fusion.60
  267.8 1.6 bitcast_reduce_fusion.2
  270.3 2.4 fusion.60
  277.9 1.6 bitcast_reduce_fusion.2
  280.5 2.4 fusion.60
  288.1 1.6 bitcast_reduce_fusion.2
  290.6 2.4 fusion.60
  298.2 1.6 bitcast_reduce_fusion.2
  300.8 2.4 fusion.60
  308.4 1.6 bitcast_reduce_fusion.2
  310.9 2.4 fusion.60
  318.5 1.6 bitcast_reduce_fusion.2
  321.1 2.4 fusion.60
  328.7 1.6 bitcast_reduce_fusion.2
  331.2 2.4 fusion.60
  338.8 1.6 bitcast_reduce_fusion.2
  341.4 2.4 fusion.60
  349.0 1.6 bitcast_reduce_fusion.2
  351.5 2.4 fusion.60
  359.1 1.6 bitcast_reduce_fusion.2
  361.7 2.4 fusion.60
  364.5 6.8 %convolution_convert_fusion = bf16[512,5120]{1,0:T(8,128)(2,1)} fusion(bf16[512,384]{0,1:T(8,128)(2,1)S(1)} %bitcast.87, bf16[384,5120]{1,0:T(8,128)(2,1)} %param.18), kind=kOutput, calls=%fused_computation.41 | convolution fusion | flops 2015887360 | bytes 9568256 | tf_op jit(solution)/shard_map/dot_general | solution.py:107
  371.3 7.9 %copy.32 = bf16[512,5120]{0,1:T(8,128)(2,1)} copy(bf16[512,5120]{1,0:T(8,128)(2,1)} %convolution_convert_fusion) | data formatting | bytes 10485760
  379.3 39.8 %reduce-scatter.4.cloned.1.call-done = bf16[640,512]{1,0:T(8,128)(2,1)} async-done(((bf16[5120,512]{1,0:T(8,128)(2,1)}), bf16[640,512]{1,0:T(8,128)(2,1)}) %reduce-scatter.4.cloned.1.call-update) | async-done | bytes 655376
  (160 shorter events, 65.5 us)
Async XLA Ops:
  6.5 41.6 %all-gather.3.cloned.1.call-start = ((), (), s32[]{:S(2)}) async-start(), calls=%async_computation.1 | async-start | bytes 5898240 | tf_op jit(solution)/shard_map/all_gather | solution.py:36
  7.3 154.1 %all-gather.5.cloned.1.call-start = ((), (), s32[]{:S(2)}) async-start(), calls=%async_computation.2 | async-start | bytes 13369344 | tf_op jit(solution)/shard_map/all_gather | solution.py:72
  48.2 4.2 copy-start
  52.4 3.0 copy-start.8
  55.5 2.7 copy-start.1
  55.5 4.0 copy-start.9
  59.5 2.3 copy-start.6
  61.7 1.5 copy-start.3
  63.0 356.1 %reduce-scatter.4.cloned.1.call-start = ((), (), s32[]{:S(2)}) async-start(), calls=%async_computation.3 | async-start | bytes 5898240
  63.9 6.3 %copy-start.7 = (f32[3,128]{1,0:T(4,128)S(1)}, f32[3,128]{1,0:T(4,128)}, u32[]{:S(2)}) copy-start(f32[3,128]{1,0:T(4,128)} %param.19) | copy-start | bytes 4612
  192.6 9.2 %copy-start.4 = (s32[1,16]{1,0:T(1,128)S(1)}, s32[1,16]{1,0:T(1,128)}, u32[]{:S(2)}) copy-start(s32[1,16]{1,0:T(1,128)} %param.24) | copy-start | bytes 196
  192.6 9.2 %copy-start.5 = (s32[16]{0:T(128)S(1)}, s32[16]{0:T(128)}, u32[]{:S(2)}) copy-start(s32[16]{0:T(128)} %param.23) | copy-start | bytes 196
  379.3 41.2 %copy-start.2 = (bf16[512,640]{1,0:T(8,128)(2,1)S(1)}, bf16[512,640]{1,0:T(8,128)(2,1)}, u32[]{:S(2)}) copy-start(bf16[512,640]{1,0:T(8,128)(2,1)} %param.14) | copy-start | bytes 1966084
Sparse Core Ops, SparseCore 0:
  9.0 39.1 all-gather.2
  63.1 98.1 all-gather.4
  379.4 39.6 reduce-scatter.3
where the time goes:
time: 431 us; the launch traced here: 428 us
  waiting for transfers between devices  170 us (39%)
  matrix products  82 us (19%)
  local copies, waits for them, and re-layouts  61.9 us (14%)
  other arithmetic  58.1 us (13%)
  loops' own time  41.6 us (10%)
  between operations  14 us (3%)
    all_gather x1, waiting for transfers between devices, on_device(): piece = lax.all_gather(kv_pair, 'frame', axis=1, tiled=True)  90.9 us
    unnamed x26, local copies, waits for them, and re-layouts  43.3 us
    another operation x1, loops' own time, on_device(): result, unused = lax.scan(fold_block, initial, blocks)  41.6 us
    unnamed x4, waiting for transfers between devices  40.6 us
    dot_general x16, matrix products, fold_block(): jnp.einsum('hqk,khd->hqd', weights.astype(jnp.bfloat16), value_block, pre...  39.2 us
    all_gather x1, waiting for transfers between devices, on_device(): lax.all_gather(latents, 'tensor', axis=1, tiled=True).astype(jnp.float32)  38.7 us
    dot_general x16, matrix products, fold_block(): jnp.einsum('qhd,khd->hqk', queries, key_block, preferred_element_type=jnp...  25.6 us
    reduce_sum x16, other arithmetic, fold_block(): linked = jnp.sum(jnp.where(span_ids == block_index, mask_row, 0)) == 1  21.5 us
  transfers between devices with their start and end apart: 3, of which 3 were waited for; matrix products, arithmetic and copies ran while one was open for 2% of the time, Pallas kernels for 0%

commit v1 on v0

--- a/solution.py
+++ b/solution.py
@@ -7,6 +7,13 @@
 HEAD_DIM = 128
 EPSILON = 1e-06
 NEG_FILL = -1e30
+
+
+def all_by_exchange(value, axis, along):
+    size = lax.axis_size(axis)
+    parts = jnp.stack([value for _ in range(size)])
+    parts = lax.all_to_all(parts, axis, split_axis=0, concat_axis=0)
+    return jnp.concatenate(parts, axis=along)
 
 
 def on_device(
@@ -33,7 +40,7 @@
     shift_row = modulation[0]
     scale_row = modulation[1]
     gate_row = modulation[2]
-    whole = lax.all_gather(latents, "tensor", axis=1, tiled=True).astype(jnp.float32)
+    whole = all_by_exchange(latents, "tensor", 1).astype(jnp.float32)
     row_mean = jnp.mean(whole, axis=1, keepdims=True)
     row_square = jnp.mean(whole * whole, axis=1, keepdims=True)
     normed = (

time: 431 us -> 482 us (1.12)
  local copies, waits for them, and re-layouts: 61.9 us -> 104 us
  starting transfers between devices: 0.26 us -> 5.82 us
    all_to_all x0 -> x1, waiting for transfers between devices: none -> 53.5 us  [all_by_exchange(): parts = lax.all_to_all(parts, axis, split_axis=0, concat_axis=0)]
    all_gather x1 -> x0, waiting for transfers between devices: 38.7 us -> none  [on_device(): lax.all_gather(latents, 'tensor', axis=1, tiled=True).astype(jnp.float32)]
    another operation x0 -> x4, local copies, waits for them, and re-layouts: none -> 37.3 us  [the longest x1 16.6 us: on_device(): key_blocks = piece[0].reshape(block_count, row_count, head_local, HEAD_DIM)]
    all_gather x1, waiting for transfers between devices: 90.9 us -> 75.2 us  [on_device(): piece = lax.all_gather(kv_pair, 'frame', axis=1, tiled=True)]
    all_to_all x0 -> x1, local copies, waits for them, and re-layouts: none -> 7.86 us  [all_by_exchange(): parts = lax.all_to_all(parts, axis, split_axis=0, concat_axis=0)]
    all_to_all x0 -> x1, starting transfers between devices: none -> 5.56 us  [all_by_exchange(): parts = lax.all_to_all(parts, axis, split_axis=0, concat_axis=0)]
    unnamed x26 -> x29, local copies, waits for them, and re-layouts: 43.3 us -> 37.9 us
    unnamed x4 -> x3, waiting for transfers between devices: 40.6 us -> 40.1 us
  transfers between devices with their start and end apart: 3 -> 3, of which waited for: 3 -> 3; matrix products, arithmetic and copies ran while one was open for 2% -> 4% of each run, Pallas kernels for 0% -> 0%
where the time goes in v1:
time: 482 us; the launch traced here: 478 us
  waiting for transfers between devices  169 us (35%)
  local copies, waits for them, and re-layouts  104 us (22%)
  matrix products  83.2 us (17%)
  other arithmetic  59.9 us (12%)
  loops' own time  42.4 us (9%)
  between operations  14.3 us (3%)
  starting transfers between devices  5.82 us (1%)
    all_gather x1, waiting for transfers between devices, on_device(): piece = lax.all_gather(kv_pair, 'frame', axis=1, tiled=True)  75.2 us
    all_to_all x1, waiting for transfers between devices, all_by_exchange(): parts = lax.all_to_all(parts, axis, split_axis=0, concat_axis=0)  53.5 us
    another operation x1, loops' own time, on_device(): result, unused = lax.scan(fold_block, initial, blocks)  42.4 us
    unnamed x3, waiting for transfers between devices  40.1 us
    dot_general x16, matrix products, fold_block(): jnp.einsum('hqk,khd->hqd', weights.astype(jnp.bfloat16), value_block, pre...  39.2 us
    unnamed x29, local copies, waits for them, and re-layouts  37.9 us
    dot_general x16, matrix products, fold_block(): jnp.einsum('qhd,khd->hqk', queries, key_block, preferred_element_type=jnp...  25.6 us
    reduce_sum x16, other arithmetic, fold_block(): linked = jnp.sum(jnp.where(span_ids == block_index, mask_row, 0)) == 1  21.5 us
  transfers between devices with their start and end apart: 3, of which 3 were waited for; matrix products, arithmetic and copies ran while one was open for 4% of the time, Pallas kernels for 0%

profile of v1, /device:TPU:0, one launch (start us, length us, event | category | flops | bytes accessed | tf_op | source)
XLA Modules:
  0.0 478.1 jit_solution(4562683713648952394)
XLA Ops:
  6.5 3.8 stack.6
  10.4 5.6 %all-to-all-start = ((bf16[8,512,640]{2,1,0:T(8,128)(2,1)}), bf16[8,512,640]{2,1,0:T(8,128)(2,1)}, u32[]{:S(2)}, u32[]{:S(2)}) async-start(bf16[8,512,640]{2,1,0:T(8,128)(2,1)} %stack.6), calls=%async_computation | async-start | bytes 10485760 | tf_op jit(solution)/shard_map/all_to_all | solution.py:15
  17.1 6.3 %copy.42 = bf16[5120,384]{0,1:T(8,128)(2,1)} copy(bf16[5120,384]{1,0:T(8,128)(2,1)} %param.16) | data formatting | bytes 7864320 | tf_op args[2]
  23.4 53.5 %all-to-all-done = bf16[8,512,640]{2,1,0:T(8,128)(2,1)} async-done(((bf16[8,512,640]{2,1,0:T(8,128)(2,1)}), bf16[8,512,640]{2,1,0:T(8,128)(2,1)}, u32[]{:S(2)}, u32[]{:S(2)}) %all-to-all-start) | async-done | bytes 5242912 | tf_op jit(solution)/shard_map/all_to_all | solution.py:15
  76.9 7.9 %copy.41 = bf16[8,512,640]{1,2,0:T(8,128)(2,1)} copy(bf16[8,512,640]{2,1,0:T(8,128)(2,1)} %all-to-all-done) | data formatting | bytes 10485760 | tf_op jit(solution)/shard_map/all_to_all | solution.py:15
  84.8 4.0 convert_reduce_fusion
  88.9 2.2 add_convert_fusion
  91.1 2.2 multiply_reduce_fusion.2
  93.7 5.1 %fusion.28 = bf16[512,5120]{0,1:T(8,128)(2,1)S(1)} fusion(bf16[8,512,640]{1,2,0:T(8,128)(2,1)} %copy.41, f32[5120]{0:T(1024)S(1)} %bitcast.91, f32[5120]{0:T(1024)S(1)} %bitcast.92, f32[512]{0:T(512)S(1)} %get-tuple-element.288, f32[512]{0:T(512)S(1)} %get-tuple-element.287), kind=kLoop, calls=%fused_computation.37 | loop fusion | flops 15728640 | bytes 10530816 | tf_op jit(solution)/shard_map/convert_element_type | solution.py:51
  98.8 2.9 fusion.29
  103.0 6.3 %copy.46 = bf16[5120,384]{0,1:T(8,128)(2,1)} copy(bf16[5120,384]{1,0:T(8,128)(2,1)} %param.15) | data formatting | bytes 7864320 | tf_op args[1]
  110.0 6.5 %multiply_reduce_fusion.1 = (f32[512,3]{0,1:T(4,128)S(1)}, f32[512,3,128]{0,2,1:T(8,128)S(1)}) fusion(bf16[512,5120,1]{0,1,2:T(8,128)(2,1)} %bitcast.85, bf16[3,128,5120]{2,1,0:T(8,128)(2,1)} %bitcast.87), kind=kOutput, calls=%fused_computation.49 | convolution fusion | flops 2013657600 | bytes 9967616 | tf_op jit(solution)/shard_map/dot_general | solution.py:55
  116.9 75.2 %all-gather.2.cloned.1.call-done = bf16[2,8192,384]{2,1,0:T(8,128)(2,1)} async-done(((bf16[2,512,384]{2,1,0:T(8,128)(2,1)}), bf16[2,8192,384]{2,1,0:T(8,128)(2,1)}) %all-gather.2.cloned.1.call-update) | async-done | bytes 12582928 | tf_op jit(solution)/shard_map/all_gather | solution.py:79
  192.1 10.4 %fusion.32 = (bf16[1,8192,384]{2,1,0:T(8,128)(2,1)}, bf16[1,8192,384]{2,1,0:T(8,128)(2,1)}) fusion(bf16[2,8192,384]{2,1,0:T(8,128)(2,1)} %all-gather.2.cloned.1.call-done), kind=kLoop, calls=%fused_computation.63 | loop fusion | bytes 25165824 | tf_op jit(solution)/shard_map/slice | solution.py:82
  202.5 16.6 %reshape.109 = bf16[16,512,3,128]{3,2,1,0:T(4,128)(2,1)} reshape(bf16[1,8192,384]{2,1,0:T(8,128)(2,1)} %get-tuple-element.282) | data formatting | bytes 12582912 | tf_op jit(solution)/shard_map/reshape;squeeze | solution.py:82
  219.1 7.9 %copy.51 = bf16[16,512,3,128]{3,1,2,0:T(8,128)(2,1)} copy(bf16[16,512,3,128]{3,2,1,0:T(4,128)(2,1)} %reshape.109) | data formatting | bytes 12582912
  227.0 16.6 %reshape.108 = bf16[16,512,3,128]{3,2,1,0:T(4,128)(2,1)} reshape(bf16[1,8192,384]{2,1,0:T(8,128)(2,1)} %get-tuple-element.283) | data formatting | bytes 12582912 | tf_op jit(solution)/shard_map/reshape;squeeze | solution.py:81
  243.6 7.7 %copy.49 = bf16[16,512,3,128]{3,1,2,0:T(8,128)(2,1)} copy(bf16[16,512,3,128]{3,2,1,0:T(4,128)(2,1)} %reshape.108) | data formatting | bytes 12582912
  251.4 162.2 %while.17 = (s32[]{:T(128)}, f32[3,512]{1,0:T(4,128)S(1)}, f32[3,512]{1,0:T(4,128)S(1)}, f32[3,512,128]{2,1,0:T(8,128)S(1)}, s32[16]{0:T(128)S(1)}, /*index=5*/s...) while((s32[]{:T(128)}, f32[3,512]{1,0:T(4,128)S(1)}, ...), condition=%wide.region_12.13_spmd.clone.clone, body=%wide.region_6.12_spmd.clone.clone.sunk | while | flops 413475456 | bytes 12295147 | solution.py:110
  256.5 1.6 bitcast_reduce_fusion.2
  259.0 2.4 fusion.55
  269.2 2.4 fusion.55
  276.8 1.6 bitcast_reduce_fusion.2
  279.3 2.4 fusion.55
  289.4 2.4 fusion.55
  297.1 1.6 bitcast_reduce_fusion.2
  299.6 2.4 fusion.55
  307.2 1.6 bitcast_reduce_fusion.2
  309.7 2.4 fusion.55
  317.3 1.6 bitcast_reduce_fusion.2
  319.9 2.4 fusion.55
  330.0 2.4 fusion.55
  337.6 1.6 bitcast_reduce_fusion.2
  340.1 2.4 fusion.55
  350.3 2.4 fusion.55
  357.9 1.6 bitcast_reduce_fusion.2
  360.4 2.4 fusion.55
  368.0 1.6 bitcast_reduce_fusion.2
  370.6 2.4 fusion.55
  378.2 1.6 bitcast_reduce_fusion.2
  380.7 2.4 fusion.55
  390.8 2.4 fusion.55
  398.5 1.6 bitcast_reduce_fusion.2
  401.0 2.4 fusion.55
  411.1 2.4 fusion.55
  414.0 6.8 %convolution_convert_fusion = bf16[512,5120]{1,0:T(8,128)(2,1)} fusion(bf16[512,384]{0,1:T(8,128)(2,1)S(1)} %bitcast.88, bf16[384,5120]{1,0:T(8,128)(2,1)} %param.18), kind=kOutput, calls=%fused_computation.41 | convolution fusion | flops 2015887360 | bytes 9568256 | tf_op jit(solution)/shard_map/dot_general | solution.py:114
  420.8 7.9 %copy.62 = bf16[512,5120]{0,1:T(8,128)(2,1)} copy(bf16[512,5120]{1,0:T(8,128)(2,1)} %convolution_convert_fusion) | data formatting | bytes 10485760
  428.8 40.0 %reduce-scatter.4.cloned.1.call-done = bf16[640,512]{1,0:T(8,128)(2,1)} async-done(((bf16[5120,512]{1,0:T(8,128)(2,1)}), bf16[640,512]{1,0:T(8,128)(2,1)}) %reduce-scatter.4.cloned.1.call-update) | async-done | bytes 655376
  (167 shorter events, 70.7 us)
Async XLA Ops:
  10.4 6.3 %copy-start.5 = (f32[16,3,5120]{2,0,1:T(8,128)S(1)}, f32[16,3,5120]{2,0,1:T(8,128)}, u32[]{:S(2)}) copy-start(f32[16,3,5120]{2,0,1:T(8,128)} %param.21) | copy-start | bytes 2949124
  10.4 66.5 %all-to-all-start = ((bf16[8,512,640]{2,1,0:T(8,128)(2,1)}), bf16[8,512,640]{2,1,0:T(8,128)(2,1)}, u32[]{:S(2)}, u32[]{:S(2)}) async-start(bf16[8,512,640]{2,1,0:T(8,128)(2,1)} %stack.6), calls=%async_computation | async-start | bytes 10485760 | tf_op jit(solution)/shard_map/all_to_all | solution.py:15
  15.9 176.1 %all-gather.2.cloned.1.call-start = ((), (), s32[]{:S(2)}) async-start(), calls=%async_computation.2 | async-start | bytes 13369344 | tf_op jit(solution)/shard_map/all_gather | solution.py:79
  84.8 4.1 copy-start
  88.8 2.2 copy-start.3
  91.0 2.3 copy-start.2
  91.1 2.3 copy-start.9
  93.7 5.1 %copy-start.1 = (bf16[5120,384]{1,0:T(8,128)(2,1)S(1)}, bf16[5120,384]{1,0:T(8,128)(2,1)}, u32[]{:S(2)}) copy-start(bf16[5120,384]{1,0:T(8,128)(2,1)} %param.17) | copy-start | bytes 11796484
  101.7 7.6 %copy-start.6 = (s32[16]{0:T(128)S(1)}, s32[16]{0:T(128)}, u32[]{:S(2)}) copy-start(s32[16]{0:T(128)} %param.25) | copy-start | bytes 196
  102.8 366.1 %reduce-scatter.4.cloned.1.call-start = ((), (), s32[]{:S(2)}) async-start(), calls=%async_computation.3 | async-start | bytes 5898240
  110.0 6.5 %copy-start.10 = (f32[3,128]{1,0:T(4,128)S(1)}, f32[3,128]{1,0:T(4,128)}, u32[]{:S(2)}) copy-start(f32[3,128]{1,0:T(4,128)} %param.19) | copy-start | bytes 4612
  243.6 7.8 %copy-start.7 = (s32[1,16]{1,0:T(1,128)S(1)}, s32[1,16]{1,0:T(1,128)}, u32[]{:S(2)}) copy-start(s32[1,16]{1,0:T(1,128)} %param.24) | copy-start | bytes 196
  243.6 7.8 %copy-start.8 = (s32[16]{0:T(128)S(1)}, s32[16]{0:T(128)}, u32[]{:S(2)}) copy-start(s32[16]{0:T(128)} %param.23) | copy-start | bytes 196
  428.7 41.5 %copy-start.4 = (bf16[512,640]{1,0:T(8,128)(2,1)S(1)}, bf16[512,640]{1,0:T(8,128)(2,1)}, u32[]{:S(2)}) copy-start(bf16[512,640]{1,0:T(8,128)(2,1)} %param.14) | copy-start | bytes 1966084
Sparse Core Ops, SparseCore 0:
  102.9 89.1 all-gather.1
  428.9 39.8 reduce-scatter.3
